TPU v7x, 512 devices: a whole 4x4x16 slice. The times are simulated.
512 devices in a mesh: gz: 64 (over y, z_hi, x, core), gy: 8 (over z_lo).
Axes of the slice: x: 4, y: 4, z: 16 (z_hi: 2, z_lo: 8; z = z_hi * 8 + z_lo), core: 2. Of those that a mesh axis runs over, the one named last changes fastest.
Arguments:
- probe_fields: float32 [1, 128, 1024, 1024], P(None, 'gz', 'gy'), may hold values from -24 to 24
- root_one: float32 [128, 1024], P('gz'), may hold values from 0.5 to 0.999
- root_two: float32 [128, 1024], P('gz'), may hold values from 0.3 to 0.8
- lateral_kernel_taps: float32 [2, 3], replicated, may hold values from 0.2 to 1
- dilations: int32 [2], replicated, may hold values from 1 to 8, as said below
Outputs:
- covariance_image: float32 [1, 128, 1024, 1024], P(None, 'gz', 'gy')
Inputs may be any that keep to these rules, and one draw needn't show every extreme that they name: `dilations`: one entry equals 8 and the other is smaller.
All inputs are finite; a program needn't handle non-finite values.
Results may differ from a plain program's by a relative error of at most 0.000044.
Values sent between devices are 32-bit elements; how exact they have to be, the bound alone decides.
A program may use at most 64 MiB of HBM per device.

v0:
```python
import functools
import jax
import jax.numpy as jnp
from jax import lax
from jax.experimental import pallas as pl
from jax.experimental.pallas import tpu as pltpu
from jax.sharding import PartitionSpec as P

MESH = pl.DeviceIdType.MESH
F32 = jnp.float32
BF16 = jnp.bfloat16
SIZES = (4, 2, 4, 2)
MARGIN = 16
QUARTERS = 4


def pieces(a):
    high = a.astype(BF16)
    return high, (a - high.astype(F32)).astype(BF16)


def dot3(a, b):
    (ah, al), (bh, bl) = a, b
    dot = functools.partial(jnp.dot, preferred_element_type=F32)
    return dot(ah, bh) + (dot(ah, bl) + dot(al, bh))


def band(shape, shift, taps, row, step):
    i = lax.broadcasted_iota(jnp.int32, shape, 0)
    j = lax.broadcasted_iota(jnp.int32, shape, 1)
    away = jnp.abs(i - j + shift)
    centre, near, far = taps[row, 0], taps[row, 1], taps[row, 2]
    weight = jnp.where(away == 0, centre, 0.0)
    weight = jnp.where(away == step, near, weight)
    weight = jnp.where(away == 2 * step, far, weight)
    return weight / (centre + 2.0 * (near + far))


def kernel(
    sizes, n_slabs, x_ref, one_ref, two_ref, taps, dils, o_ref,
    send, recv, back, roots_s, roots_r, first, second, gain, above, below,
    kx_high, kx_low, trans, spread, ends, starts, ends2, starts2,
    root_sem, halo_sem, out_sem, in_sem, trans_sem, end_sem, end2_sem, home_s, home_r,
):
    ny, nz, nxx, nc = sizes
    group = ny * nxx * nc
    block = nxx * nc * 2
    rows = recv.shape[3]
    g, gy = lax.axis_index("gz"), lax.axis_index("gy")
    core, col = lax.rem(g, nc), lax.rem(g // nc, nxx)
    half, line = lax.rem(g // (nc * nxx), nz), g // (nc * nxx * nz)
    me = (line * nxx + col) * nc + core
    partner = ((line * nz + (1 - half)) * nxx + col) * nc + core

    def reach(n, step):
        return min(step, n - step)

    steps = [(a, b, c) for a in range(ny) for b in range(nxx) for c in range(nc)][1:]
    steps.sort(key=lambda s: (-reach(ny, s[0]) - reach(nxx, s[1]), -min(s[0], 1) - min(s[1], 1)))

    def peers():
        for a, b, c in steps:
            yy, xx, cc = lax.rem(line + a, ny), lax.rem(col + b, nxx), lax.rem(core + c, nc)
            yield ((yy * nz + half) * nxx + xx) * nc + cc, (yy * nxx + xx) * nc + cc

    def remote(src, dst, s, r, gz, slab=gy):
        return pltpu.make_async_remote_copy(
            src, dst, s, r, device_id=(gz, slab), device_id_type=MESH
        )

    def arrived(ref, sem):
        pltpu.make_async_copy(ref, ref, sem).wait()

    has_up, has_down = gy > 0, gy < n_slabs - 1

    barrier = pltpu.get_barrier_semaphore()

    def hello(gz, slab):
        pl.semaphore_signal(barrier, inc=1, device_id=(gz, slab), device_id_type=MESH)

    hello(partner, gy)

    @pl.when(has_up)
    def _():
        hello(g, gy - 1)

    @pl.when(has_down)
    def _():
        hello(g, gy + 1)

    for gz, _ in peers():
        hello(gz, gy)

    for p in range(2):
        for q in range(QUARTERS):
            lanes = slice(256 * q, 256 * q + 256)
            roots_s[p, q : q + 1, :] = one_ref[p : p + 1, lanes]
            roots_s[p, 4 + q : 5 + q, :] = two_ref[p : p + 1, lanes]

    def to_quarters(c, p, at, value):
        n = value.shape[0]
        for q in range(QUARTERS):
            for h in range(2):
                lanes = slice(256 * q + 128 * h, 256 * q + 128 * h + 128)
                send[c, p, h, pl.ds(at * QUARTERS + q, n, stride=QUARTERS), :] = value[:, lanes]

    ky = functools.partial(band, taps=taps, row=1, step=dils[1])
    exact = functools.partial(jnp.dot, precision=lax.Precision.HIGHEST, preferred_element_type=F32)
    inner = pieces(exact(ky((64, 96), MARGIN), ky((96, 128), MARGIN)))
    for p in range(2):
        to_quarters(0, p, 0, dot3(inner, pieces(x_ref[p])))

    pl.semaphore_wait(
        barrier, group + has_up.astype(jnp.int32) + has_down.astype(jnp.int32)
    )

    up = remote(x_ref.at[:, 0:32], below, halo_sem.at[0], halo_sem.at[2], g, gy - 1)
    down = remote(x_ref.at[:, 96:128], above, halo_sem.at[1], halo_sem.at[3], g, gy + 1)

    @pl.when(has_up)
    def _():
        up.start()

    @pl.when(has_down)
    def _():
        down.start()

    for gz, _ in peers():
        remote(roots_s, roots_r.at[pl.ds(2 * me, 2)], root_sem.at[0], root_sem.at[1], gz).start()

    def spread_rows(c):
        for gz, place in peers():
            remote(
                send.at[c, :, :, pl.ds(pl.multiple_of(place * rows, 8), rows)],
                recv.at[c, pl.ds(2 * me, 2)],
                out_sem.at[c], in_sem.at[c], gz,
            ).start()

        recv[c, pl.ds(2 * me, 2)] = send[c, :, :, pl.ds(pl.multiple_of(me * rows, 8), rows)]

    spread_rows(0)
    roots_r[pl.ds(2 * me, 2)] = roots_s[...]
    kx = band((512, 256), -128, taps, 0, dils[0])
    kx_high[...], kx_low[...] = pieces(kx)

    arrived(roots_r.at[pl.ds(0, 2 * group - 2)], root_sem.at[1])
    sub = lax.broadcasted_iota(jnp.int32, (8, 256), 0)

    @pl.loop(0, 2 * group)
    def _(k):
        both = roots_r[k]
        turned = pltpu.roll(both, 4, 0)
        one, two = jnp.where(sub < 4, both, turned), jnp.where(sub < 4, turned, both)
        first[k], second[k] = one + two, -one * two
        gain[k] = (1.0 - one) * (1.0 - two)

    def advance(k, states):
        out = []
        for b, (y1, y2) in enumerate(states):
            at = b * block + k
            out.append((first[at] * y1 + second[at] * y2, y1))
        return tuple(out)

    unit = (jnp.where(sub < 4, 1.0, 0.0), jnp.where(sub < 4, 0.0, 1.0))
    done = advance(1, advance(0, [unit] * ny))
    done = lax.fori_loop(2, block, advance, done)
    for b, (y1, y2) in enumerate(done):
        trans[half, b, 0] = y1
        trans[half, b, 1] = y2
    trans_copy = remote(trans.at[half], trans.at[half], trans_sem.at[0], trans_sem.at[1], partner)
    trans_copy.start()

    @pl.when(has_up)
    def _():
        down.wait_recv()

    @pl.when(jnp.logical_not(has_up))
    def _():
        above[...] = jnp.zeros_like(above)

    @pl.when(has_down)
    def _():
        up.wait_recv()

    @pl.when(jnp.logical_not(has_down))
    def _():
        below[...] = jnp.zeros_like(below)

    mid = lax.broadcasted_iota(jnp.int32, (64, 96), 0)
    head, tail = ky((32, 64), MARGIN), ky((64, 96), MARGIN)
    top = pieces(exact(head, jnp.where(has_up | (mid >= MARGIN), tail, 0.0)))
    bottom = pieces(exact(head, jnp.where(has_down | (mid < 64 - MARGIN), tail, 0.0)))
    for p in range(2):
        over = jnp.concatenate([above[p], x_ref[p, 0:64]], 0)
        to_quarters(1, p, 0, dot3(top, pieces(over)))
        under = jnp.concatenate([x_ref[p, 64:128], below[p]], 0)
        to_quarters(1, p, 32, dot3(bottom, pieces(under)))
    spread_rows(1)

    def load(c, k):
        return jnp.concatenate([recv[c, k, 0], recv[c, k, 1]], -1)

    def store(c, k, value):
        recv[c, k, 0] = value[:, :128]
        recv[c, k, 1] = value[:, 128:]

    def back_scan(c, begin, keep):
        def step(i, states):
            out = []
            for b, (u, t) in enumerate(states):
                at = b * block + block - 1 - i
                z = load(c, at) + u
                if keep:
                    store(c, at, gain[at] * z)
                out.append((first[at] * z + t, second[at] * z))
            return tuple(out)

        return lax.fori_loop(2, block, step, step(1, step(0, begin)))

    def fore_scan(c, begin, keep):
        def step(k, states):
            out = []
            for b, (y1, y2) in enumerate(states):
                at = b * block + k
                y = gain[at] * load(c, at) + first[at] * y1 + second[at] * y2
                if keep:
                    store(c, at, y)
                out.append((y, y1))
            return tuple(out)

        return lax.fori_loop(2, block, step, step(1, step(0, begin)))

    zero = jnp.zeros((rows, 256), F32)
    nothing = [(zero, zero)] * ny

    def hand_over(buf, sems, c, states):
        for b, (s1, s2) in enumerate(states):
            buf[c, half, b, 0] = s1
            buf[c, half, b, 1] = s2
        remote(
            buf.at[c, half], buf.at[c, half], sems.at[0, c], sems.at[1, c], partner
        ).start()

    def x_twice(c):
        @pl.loop(0, ny)
        def _(b):
            n = block * rows
            quarter = lax.rem(lax.broadcasted_iota(jnp.int32, (n, 128), 0), QUARTERS)
            at = pl.ds(b * block, block)
            left = recv[c, at, 0].reshape(n, 128)
            right = recv[c, at, 1].reshape(n, 128)
            matrix = (kx_high[...], kx_low[...])
            for _ in range(2):
                before = jnp.where(quarter == 0, 0.0, pltpu.roll(right, 1, 0))
                after = jnp.where(quarter == 3, 0.0, pltpu.roll(left, n - 1, 0))
                whole = dot3(pieces(jnp.concatenate([before, left, right, after], 1)), matrix)
                left, right = whole[:, :128], whole[:, 128:]
            recv[c, at, 0] = left.reshape(block, rows, 128)
            recv[c, at, 1] = right.reshape(block, rows, 128)

    for c in range(2):
        arrived(recv.at[c, pl.ds(0, 2 * group - 2)], in_sem.at[c])
        hand_over(ends, end_sem, c, back_scan(c, nothing, False))

    trans_copy.wait_recv()
    for z in range(nz):
        for b in range(ny):
            for s in range(2):
                a = trans[z, b, s]
                turned = pltpu.roll(a, 4, 0)
                spread[z, b, s, 0] = jnp.where(sub < 4, a, turned)
                spread[z, b, s, 1] = jnp.where(sub < 4, turned, a)

    for c in range(2):
        arrived(ends.at[c, 1 - half], end_sem.at[1, c])
        u, t = zero, zero
        for j in reversed(range(ny * nz)):
            b, z = j // nz, j % nz
            starts[c, z, b, 0], starts[c, z, b, 1] = u, t
            u, t = (
                spread[z, b, 0, 0] * u + spread[z, b, 1, 0] * t + ends[c, z, b, 0],
                spread[z, b, 0, 1] * u + spread[z, b, 1, 1] * t + ends[c, z, b, 1],
            )
        begin = [(starts[c, half, b, 0], starts[c, half, b, 1]) for b in range(ny)]
        back_scan(c, begin, True)
        x_twice(c)
        hand_over(ends2, end2_sem, c, fore_scan(c, nothing, False))

    for c in range(2):
        arrived(ends2.at[c, 1 - half], end2_sem.at[1, c])
        y1, y2 = zero, zero
        for j in range(ny * nz):
            b, z = j // nz, j % nz
            starts2[c, z, b, 0], starts2[c, z, b, 1] = y1, y2
            y1, y2 = (
                spread[z, b, 0, 0] * y1 + spread[z, b, 0, 1] * y2 + ends2[c, z, b, 0],
                spread[z, b, 1, 0] * y1 + spread[z, b, 1, 1] * y2 + ends2[c, z, b, 1],
            )
        begin = [(starts2[c, half, b, 0], starts2[c, half, b, 1]) for b in range(ny)]
        fore_scan(c, begin, True)

        for gz, place in peers():
            remote(
                recv.at[c, pl.ds(2 * place, 2)],
                back.at[c, :, :, pl.ds(pl.multiple_of(me * rows, 8), rows)],
                home_s.at[c], home_r.at[c], gz,
            ).start()

        back[c, :, :, pl.ds(pl.multiple_of(me * rows, 8), rows)] = recv[c, pl.ds(2 * me, 2)]

    for c in range(2):
        arrived(back.at[c, :, :, pl.ds(0, (group - 1) * rows)], home_r.at[c])
        for p in range(2):
            for q in range(QUARTERS):
                for h in range(2):
                    lanes = slice(256 * q + 128 * h, 256 * q + 128 * h + 128)
                    for at, to, n in ((0, 32, 64),) if c == 0 else ((0, 0, 32), (32, 96, 32)):
                        o_ref[p, to : to + n, lanes] = back[
                            c, p, h, pl.ds(at * QUARTERS + q, n, stride=QUARTERS), :
                        ]

    @pl.when(has_up)
    def _():
        up.wait_send()

    @pl.when(has_down)
    def _():
        down.wait_send()

    trans_copy.wait_send()
    arrived(roots_r.at[pl.ds(0, 2 * group - 2)], root_sem.at[0])
    for c in range(2):
        arrived(send.at[c, :, :, pl.ds(0, (group - 1) * rows)], out_sem.at[c])
        arrived(ends.at[c, 0], end_sem.at[0, c])
        arrived(ends2.at[c, 0], end2_sem.at[0, c])
        arrived(back.at[c, :, :, pl.ds(0, (group - 1) * rows)], home_s.at[c])


def build(sizes, n_slabs):
    ny, nz, nxx, nc = sizes
    group = ny * nxx * nc
    rows = 64 // group * QUARTERS

    def body(probe_fields, root_one, root_two, lateral_kernel_taps, dilations):
        vmem, smem = (pl.BlockSpec(memory_space=s) for s in (pltpu.VMEM, pltpu.SMEM))
        dma = pltpu.SemaphoreType.DMA
        out = pl.pallas_call(
            functools.partial(kernel, sizes, n_slabs),
            out_shape=jax.ShapeDtypeStruct((2, 128, 1024), F32),
            in_specs=[vmem, vmem, vmem, smem, smem],
            out_specs=vmem,
            scratch_shapes=[
                pltpu.VMEM((2, 2, 2, 256, 128), F32),
                pltpu.VMEM((2, 2 * group, 2, rows, 128), F32),
                pltpu.VMEM((2, 2, 2, 256, 128), F32),
                pltpu.VMEM((2, 8, 256), F32),
                pltpu.VMEM((2 * group, 8, 256), F32),
                pltpu.VMEM((2 * group, 8, 256), F32),
                pltpu.VMEM((2 * group, 8, 256), F32),
                pltpu.VMEM((2 * group, 8, 256), F32),
                pltpu.VMEM((2, 32, 1024), F32),
                pltpu.VMEM((2, 32, 1024), F32),
                pltpu.VMEM((512, 256), BF16),
                pltpu.VMEM((512, 256), BF16),
                pltpu.VMEM((nz, ny, 2, 8, 256), F32),
                pltpu.VMEM((nz, ny, 2, 2, 8, 256), F32),
                pltpu.VMEM((2, nz, ny, 2, rows, 256), F32),
                pltpu.VMEM((2, nz, ny, 2, rows, 256), F32),
                pltpu.VMEM((2, nz, ny, 2, rows, 256), F32),
                pltpu.VMEM((2, nz, ny, 2, rows, 256), F32),
                dma((2,)),
                dma((4,)),
                dma((2,)),
                dma((2,)),
                dma((2,)),
                dma((2, 2)),
                dma((2, 2)),
                dma((2,)),
                dma((2,)),
            ],
            compiler_params=pltpu.CompilerParams(
                collective_id=0, has_side_effects=True, vmem_limit_bytes=48 << 20
            ),
        )(probe_fields[0], root_one, root_two, lateral_kernel_taps, dilations)
        return out[None]

    return body


def solution(mesh):
    placed = (P(None, "gz", "gy", None), P("gz", None), P("gz", None), P(), P())
    return jax.shard_map(
        build(SIZES, mesh.shape["gy"]),
        mesh=mesh,
        in_specs=placed,
        out_specs=P(None, "gz", "gy", None),
        check_vma=False,
    )
```

profile of v0, /device:TPU:67, one launch (start us, length us, event | category | flops | bytes accessed | tf_op | source)
XLA Modules:
  0.0 81.4 jit_solution(17170921001149554969)
XLA Ops:
  0.0 0.0 copy-start.4
  0.0 0.0 copy-start.3
  0.0 0.7 copy-done.4
  0.7 0.0 copy-done.3
  0.7 0.0 copy-start
  0.7 1.2 %copy-done = f32[1,2,128,1024]{3,2,1,0:T(8,128)S(1)} copy-done((f32[1,2,128,1024]{3,2,1,0:T(8,128)S(1)}, f32[1,2,128,1024]{3,2,1,0:T(8,128)}, u32[]{:S(2)}) %copy-start) | copy-done | bytes 1048600
  1.9 0.0 copy-start.1
  1.9 0.7 copy-done.1
  2.6 0.0 copy-start.2
  2.6 0.7 copy-done.2
  3.3 77.1 %shard_map.55 = f32[2,128,1024]{2,1,0:T(8,128)S(1)} custom-call(f32[2,128,1024]{2,1,0:T(8,128)S(1)} %bitcast.3, f32[2,1024]{1,0:T(2,128)S(1)} %copy-done.1, f32[2,1024]{1,0:T(2,128)S(1)} %copy-done.2, f32[2,3]{1,0:T(2,128)S(1)} %copy-done.3, s32[2]{0:T(128)S(1)} %copy-done.4), custom_call_target="tpu_custom_call" | custom-call | tf_op jit(solution)/shard_map/pallas_call | solution.py:347
  80.4 1.0 %copy.7 = f32[1,2,128,1024]{3,2,1,0:T(8,128)} copy(f32[1,2,128,1024]{3,2,1,0:T(8,128)S(1)} %bitcast.2) | data formatting | bytes 2097152
Async XLA Ops:
  0.0 0.7 copy-start.4
  0.0 0.7 copy-start.3
  0.7 1.2 %copy-start = (f32[1,2,128,1024]{3,2,1,0:T(8,128)S(1)}, f32[1,2,128,1024]{3,2,1,0:T(8,128)}, u32[]{:S(2)}) copy-start(f32[1,2,128,1024]{3,2,1,0:T(8,128)} %param.5) | copy-start | bytes 3145732
  1.9 0.7 copy-start.1
  2.6 0.7 copy-start.2
where the time goes:
time: 81.7 us; the launch traced here: 81.4 us
  Pallas kernels  77.1 us (94%)
  local copies, waits for them, and re-layouts  4.28 us (5%)
    pallas_call x1, Pallas kernels, body(): pl.pallas_call(functools.partial(kernel, sizes, n_slabs), out_shape=jax.S...  77.1 us
    unnamed x11, local copies, waits for them, and re-layouts  4.28 us

commit v1 on v0

v1 whole, which is shorter than its diff:
```python
import functools
import jax
import jax.numpy as jnp
from jax import lax
from jax.experimental import pallas as pl
from jax.experimental.pallas import tpu as pltpu
from jax.sharding import PartitionSpec as P

MESH = pl.DeviceIdType.MESH
F32 = jnp.float32
BF16 = jnp.bfloat16
SIZES = (4, 2, 4, 2)
MARGIN = 16
EIGHTHS = 8
RUNS = (32, 64, 0, 96)
CHUNKS = ((0, 1), (1, 1), (2, 1), (3, 1))


def pieces(a):
    high = a.astype(BF16)
    return high, (a - high.astype(F32)).astype(BF16)


def dot3(a, b):
    (ah, al), (bh, bl) = a, b
    dot = functools.partial(jnp.dot, preferred_element_type=F32)
    return dot(ah, bh) + (dot(ah, bl) + dot(al, bh))


def stencil(away, taps, row, step):
    centre, near, far = taps[row, 0], taps[row, 1], taps[row, 2]
    weight = jnp.where(away == 0, centre, 0.0)
    weight = jnp.where(away == step, near, weight)
    weight = jnp.where(away == 2 * step, far, weight)
    return weight / (centre + 2.0 * (near + far))


def kernel(
    sizes, n_slabs, x_hbm, one_hbm, two_hbm, taps_hbm, dils_hbm, o_ref,
    x_ref, one_ref, two_ref, taps, dils, send, recv, back, roots_s, roots_r, first, second, gain,
    above, below, kx_high, kx_low, trans, ends, ends2, starts,
    load_sem, root_sem, halo_sem, out_sem, in_sem, trans_sem, end_sem, end2_sem, home_s, home_r,
):
    ny, nz, nxx, nc = sizes
    chips = ny * nxx
    group = chips * nc
    block = nxx * nc * 2
    g, gy = lax.axis_index("gz"), lax.axis_index("gy")
    core, col = lax.rem(g, nc), lax.rem(g // nc, nxx)
    half, line = lax.rem(g // (nc * nxx), nz), g // (nc * nxx * nz)
    chip = line * nxx + col
    me = chip * nc + core

    def gz_of(yy, zz, xx, cc):
        return ((yy * nz + zz) * nxx + xx) * nc + cc

    partner, sibling = gz_of(line, 1 - half, col, core), gz_of(line, half, col, 1 - core)

    def reach(n, step):
        return min(step, n - step)

    steps = [(a, b, c) for a in range(ny) for b in range(nxx) for c in range(nc)][1:]
    steps.sort(key=lambda s: (-reach(ny, s[0]) - reach(nxx, s[1]), -min(s[0], 1) - min(s[1], 1)))

    def peers(same_core=False):
        for a, b, c in steps:
            if same_core and c:
                continue
            yy, xx, cc = lax.rem(line + a, ny), lax.rem(col + b, nxx), lax.rem(core + c, nc)
            yield gz_of(yy, half, xx, cc), (yy * nxx + xx) * nc + cc

    def remote(src, dst, s, r, gz, slab=gy):
        return pltpu.make_async_remote_copy(
            src, dst, s, r, device_id=(gz, slab), device_id_type=MESH
        )

    def arrived(ref, sem):
        pltpu.make_async_copy(ref, ref, sem).wait()

    def flat(place):
        return pl.ds(pl.multiple_of(place * EIGHTHS, EIGHTHS), EIGHTHS)

    loads = [
        pltpu.make_async_copy(a, b, load_sem.at[i])
        for i, (a, b) in enumerate(
            (
                (one_hbm, one_ref),
                (two_hbm, two_ref),
                (taps_hbm, taps),
                (dils_hbm, dils),
                (x_hbm, x_ref),
            )
        )
    ]
    for copy in loads:
        copy.start()

    has_up, has_down = gy > 0, gy < n_slabs - 1

    barrier = pltpu.get_barrier_semaphore()

    def hello(gz, slab):
        pl.semaphore_signal(barrier, inc=1, device_id=(gz, slab), device_id_type=MESH)

    hello(partner, gy)

    @pl.when(has_up)
    def _():
        hello(g, gy - 1)

    @pl.when(has_down)
    def _():
        hello(g, gy + 1)

    for gz, _ in peers():
        hello(gz, gy)

    loads[0].wait()
    loads[1].wait()
    for p in range(2):
        for e in range(EIGHTHS):
            lanes = slice(128 * e, 128 * e + 128)
            roots_s[p, 0, e : e + 1, :] = one_ref[p : p + 1, lanes]
            roots_s[p, 1, e : e + 1, :] = two_ref[p : p + 1, lanes]

    loads[2].wait()
    loads[3].wait()
    exact = functools.partial(jnp.dot, precision=lax.Precision.HIGHEST, preferred_element_type=F32)

    def ky(n_out, n_in):
        i = lax.broadcasted_iota(jnp.int32, (n_out, n_in), 0)
        j = lax.broadcasted_iota(jnp.int32, (n_out, n_in), 1)
        return stencil(jnp.abs(i - j + MARGIN), taps, 1, dils[1])

    def to_flat(slot, p, value):
        for e in range(EIGHTHS):
            send[slot, p, pl.ds(e, 32, stride=EIGHTHS), :] = value[:, 128 * e : 128 * e + 128]

    inner = pieces(exact(ky(64, 96), ky(96, 128)))
    loads[4].wait()
    for p in range(2):
        middle = dot3(inner, pieces(x_ref[p]))
        to_flat(0, p, middle[:32])
        to_flat(1, p, middle[32:])

    pl.semaphore_wait(
        barrier, group + has_up.astype(jnp.int32) + has_down.astype(jnp.int32)
    )

    for gz, _ in peers(True):
        remote(roots_s, roots_r.at[core, chip], root_sem.at[0], root_sem.at[1], gz).start()
    up = remote(x_ref.at[:, 0:32], below, halo_sem.at[0], halo_sem.at[2], g, gy - 1)
    down = remote(x_ref.at[:, 96:128], above, halo_sem.at[1], halo_sem.at[3], g, gy + 1)

    @pl.when(has_up)
    def _():
        up.start()

    @pl.when(has_down)
    def _():
        down.start()

    def spread_rows(n):
        at = pl.ds(*CHUNKS[n])
        for gz, place in peers():
            remote(
                send.at[at, :, flat(place)], recv.at[at, pl.ds(2 * me, 2)],
                out_sem.at[n], in_sem.at[n], gz,
            ).start()
        recv[at, pl.ds(2 * me, 2)] = send[at, :, flat(me)]

    inner_chunks = [n for n, (s, _) in enumerate(CHUNKS) if s < 2]
    outer_chunks = [n for n, (s, _) in enumerate(CHUNKS) if s >= 2]
    for n in inner_chunks:
        spread_rows(n)
    roots_r[core, chip] = roots_s[...]

    i = lax.broadcasted_iota(jnp.int32, (256, 128), 0)
    j = lax.broadcasted_iota(jnp.int32, (256, 128), 1)
    kx = stencil(jnp.abs(jnp.where(i < 192, i, i - 256) - j), taps, 0, dils[0])
    kx_high[...], kx_low[...] = pieces(kx)

    arrived(roots_r.at[0, pl.ds(0, chips - 1)], root_sem.at[1])
    root_copy = remote(
        roots_r.at[core], roots_r.at[core], root_sem.at[2], root_sem.at[3], sibling
    )
    root_copy.start()

    head, tail = ky(32, 64), ky(64, 96)
    mid = lax.broadcasted_iota(jnp.int32, (64, 96), 0)
    top = pieces(exact(head, jnp.where(has_up | (mid >= MARGIN), tail, 0.0)))
    bottom = pieces(exact(head, jnp.where(has_down | (mid < 64 - MARGIN), tail, 0.0)))

    root_copy.wait_recv()

    @pl.loop(0, 2 * group)
    def _(k):
        c, ch, p = lax.rem(k // 2, nc), k // (2 * nc), lax.rem(k, 2)
        one, two = roots_r[c, ch, p, 0], roots_r[c, ch, p, 1]
        first[k], second[k] = one + two, -one * two
        gain[k] = (1.0 - one) * (1.0 - two)

    def advance(k, states):
        out = []
        for b in range(ny):
            at = b * block + k
            f, s = first[at], second[at]
            out.append(tuple((f * y1 + s * y2, y1) for y1, y2 in states[b]))
        return tuple(out)

    begin = []
    for b in range(ny):
        f0, s0, f1, s1 = first[b * block], second[b * block], first[b * block + 1], second[b * block + 1]
        begin.append(((f1 * f0 + s1, f0), (f1 * s0, s0)))
    done = lax.fori_loop(2, block, advance, tuple(begin))
    for b in range(ny):
        (a, c), (d, e) = done[b]
        for n, value in enumerate((a, d, c, e)):
            trans[half, 4 * b + n] = value
    trans_copy = remote(
        trans.at[half, chip], trans.at[half, chip], trans_sem.at[0], trans_sem.at[1], partner
    )
    trans_copy.start()

    @pl.when(has_up)
    def _():
        down.wait_recv()

    @pl.when(jnp.logical_not(has_up))
    def _():
        above[...] = jnp.zeros_like(above)

    @pl.when(has_down)
    def _():
        up.wait_recv()

    @pl.when(jnp.logical_not(has_down))
    def _():
        below[...] = jnp.zeros_like(below)

    for p in range(2):
        over = jnp.concatenate([above[p], x_ref[p, 0:64]], 0)
        to_flat(2, p, dot3(top, pieces(over)))
    for n in outer_chunks[:1]:
        if len(outer_chunks) == 2:
            spread_rows(n)
    for p in range(2):
        under = jnp.concatenate([x_ref[p, 64:128], below[p]], 0)
        to_flat(3, p, dot3(bottom, pieces(under)))
    spread_rows(outer_chunks[-1])

    def back_scan(slot, begin, keep):
        def step(i, states):
            out = []
            for b, (u, t) in enumerate(states):
                at = b * block + block - 1 - i
                z = recv[slot, at] + u
                if keep:
                    recv[slot, at] = gain[at] * z
                out.append((first[at] * z + t, second[at] * z))
            return tuple(out)

        return lax.fori_loop(2, block, step, step(1, step(0, begin)))

    def fore_scan(slot, begin, keep):
        def step(k, states):
            out = []
            for b, (y1, y2) in enumerate(states):
                at = b * block + k
                y = gain[at] * recv[slot, at] + first[at] * y1 + second[at] * y2
                if keep:
                    recv[slot, at] = y
                out.append((y, y1))
            return tuple(out)

        return lax.fori_loop(2, block, step, step(1, step(0, begin)))

    zero = jnp.zeros((EIGHTHS, 128), F32)
    nothing = [(zero, zero)] * ny

    def slots(n):
        return range(CHUNKS[n][0], sum(CHUNKS[n]))

    def hand_over(buf, sems, n, scan):
        for slot in slots(n):
            for b, (s1, s2) in enumerate(scan(slot, nothing, False)):
                buf[slot, half, b, 0] = s1
                buf[slot, half, b, 1] = s2
        at = pl.ds(*CHUNKS[n])
        remote(
            buf.at[at, half], buf.at[at, half], sems.at[0, n], sems.at[1, n], partner
        ).start()

    def x_twice(slot):
        n = 2 * group * EIGHTHS
        eighth = lax.rem(lax.broadcasted_iota(jnp.int32, (n, 128), 0), EIGHTHS)
        lane = lax.broadcasted_iota(jnp.int32, (n, 128), 1)
        own = recv[slot].reshape(n, 128)
        matrix = (kx_high[...], kx_low[...])
        for _ in range(2):
            before = jnp.where(eighth == 0, 0.0, pltpu.roll(own, 1, 0))
            after = jnp.where(eighth == EIGHTHS - 1, 0.0, pltpu.roll(own, n - 1, 0))
            sides = jnp.where(lane < 64, after, before)
            own = dot3(pieces(jnp.concatenate([own, sides], 1)), matrix)
        recv[slot] = own.reshape(2 * group, EIGHTHS, 128)

    def far_state(buf, n):
        arrived(buf.at[pl.ds(*CHUNKS[n]), 1 - half], (end_sem if buf is ends else end2_sem).at[1, n])

    for n in range(len(CHUNKS)):
        arrived(recv.at[pl.ds(*CHUNKS[n]), pl.ds(0, 2 * group - 2)], in_sem.at[n])
        hand_over(ends, end_sem, n, back_scan)
        if n == 0:
            trans_copy.wait_recv()
            for gz, _ in peers(True):
                remote(
                    trans.at[1 - half, chip], trans.at[1 - half, chip],
                    trans_sem.at[2], trans_sem.at[3], gz,
                ).start()

    arrived(trans.at[1 - half, pl.ds(0, chips - 1)], trans_sem.at[3])

    for n in range(len(CHUNKS)):
        far_state(ends, n)
        for slot in slots(n):
            u, t = zero, zero
            for j in reversed(range(ny * nz)):
                b, z = j // nz, j % nz
                starts[slot, z, b, 0], starts[slot, z, b, 1] = u, t
                a11, a12, a21, a22 = (trans[z, 4 * b + i] for i in range(4))
                u, t = a11 * u + a21 * t + ends[slot, z, b, 0], a12 * u + a22 * t + ends[slot, z, b, 1]
            begin = [(starts[slot, half, b, 0], starts[slot, half, b, 1]) for b in range(ny)]
            back_scan(slot, begin, True)
            x_twice(slot)
        hand_over(ends2, end2_sem, n, fore_scan)

    for n in range(len(CHUNKS)):
        far_state(ends2, n)
        for slot in slots(n):
            y1, y2 = zero, zero
            for j in range(ny * nz):
                b, z = j // nz, j % nz
                starts[slot, z, b, 0], starts[slot, z, b, 1] = y1, y2
                a11, a12, a21, a22 = (trans[z, 4 * b + i] for i in range(4))
                y1, y2 = (
                    a11 * y1 + a12 * y2 + ends2[slot, z, b, 0],
                    a21 * y1 + a22 * y2 + ends2[slot, z, b, 1],
                )
            begin = [(starts[slot, half, b, 0], starts[slot, half, b, 1]) for b in range(ny)]
            fore_scan(slot, begin, True)
        at = pl.ds(*CHUNKS[n])
        for gz, place in peers():
            remote(
                recv.at[at, pl.ds(2 * place, 2)], back.at[at, :, flat(me)],
                home_s.at[n], home_r.at[n], gz,
            ).start()
        back[at, :, flat(me)] = recv[at, pl.ds(2 * me, 2)]

    for n in range(len(CHUNKS)):
        arrived(back.at[pl.ds(*CHUNKS[n]), :, pl.ds(0, (group - 1) * EIGHTHS)], home_r.at[n])
        for slot in slots(n):
            to = RUNS[slot]
            for p in range(2):
                for e in range(EIGHTHS):
                    o_ref[p, to : to + 32, 128 * e : 128 * e + 128] = back[
                        slot, p, pl.ds(e, 32, stride=EIGHTHS), :
                    ]

    @pl.when(has_up)
    def _():
        up.wait_send()

    @pl.when(has_down)
    def _():
        down.wait_send()

    trans_copy.wait_send()
    root_copy.wait_send()
    arrived(trans.at[1 - half, pl.ds(0, chips - 1)], trans_sem.at[2])
    arrived(roots_r.at[0, pl.ds(0, chips - 1)], root_sem.at[0])
    for n in range(len(CHUNKS)):
        at = pl.ds(*CHUNKS[n])
        arrived(send.at[at, :, pl.ds(0, (group - 1) * EIGHTHS)], out_sem.at[n])
        arrived(ends.at[at, 0], end_sem.at[0, n])
        arrived(ends2.at[at, 0], end2_sem.at[0, n])
        arrived(back.at[at, :, pl.ds(0, (group - 1) * EIGHTHS)], home_s.at[n])


def build(sizes, n_slabs):
    ny, nz, nxx, nc = sizes
    chips = ny * nxx
    group = chips * nc
    steps = len(CHUNKS)

    def body(probe_fields, root_one, root_two, lateral_kernel_taps, dilations):
        dma, vmem, smem = pltpu.SemaphoreType.DMA, pltpu.VMEM, pltpu.SMEM
        out = pl.pallas_call(
            functools.partial(kernel, sizes, n_slabs),
            out_shape=jax.ShapeDtypeStruct((2, 128, 1024), F32),
            in_specs=[pl.BlockSpec(memory_space=pltpu.HBM)] * 5,
            out_specs=pl.BlockSpec(memory_space=vmem),
            scratch_shapes=[
                vmem((2, 128, 1024), F32),
                vmem((2, 1024), F32),
                vmem((2, 1024), F32),
                smem((2, 3), F32),
                smem((2,), jnp.int32),
                vmem((4, 2, 256, 128), F32),
                vmem((4, 2 * group, 8, 128), F32),
                vmem((4, 2, 256, 128), F32),
                vmem((2, 2, 8, 128), F32),
                vmem((nc, chips, 2, 2, 8, 128), F32),
                vmem((2 * group, 8, 128), F32),
                vmem((2 * group, 8, 128), F32),
                vmem((2 * group, 8, 128), F32),
                vmem((2, 32, 1024), F32),
                vmem((2, 32, 1024), F32),
                vmem((256, 128), BF16),
                vmem((256, 128), BF16),
                vmem((nz, 4 * ny, 8, 128), F32),
                vmem((4, nz, ny, 2, 8, 128), F32),
                vmem((4, nz, ny, 2, 8, 128), F32),
                vmem((4, nz, ny, 2, 8, 128), F32),
                dma((5,)),
                dma((4,)),
                dma((4,)),
                dma((steps,)),
                dma((steps,)),
                dma((4,)),
                dma((2, steps)),
                dma((2, steps)),
                dma((steps,)),
                dma((steps,)),
            ],
            compiler_params=pltpu.CompilerParams(
                collective_id=0, has_side_effects=True, vmem_limit_bytes=48 << 20
            ),
        )(probe_fields[0], root_one, root_two, lateral_kernel_taps, dilations)
        return out[None]

    return body


def solution(mesh):
    placed = (P(None, "gz", "gy", None), P("gz", None), P("gz", None), P(), P())
    return jax.shard_map(
        build(SIZES, mesh.shape["gy"]),
        mesh=mesh,
        in_specs=placed,
        out_specs=P(None, "gz", "gy", None),
        check_vma=False,
    )
```

time: 81.7 us -> 72.5 us (0.89)
  the two profiles are of different devices: /device:TPU:67 before, /device:TPU:1 now
where the time goes in v1:
time: 72.5 us; the launch traced here: 72.2 us
  Pallas kernels  67.9 us (94%)
  local copies, waits for them, and re-layouts  4.28 us (6%)
    pallas_call x1, Pallas kernels, body(): pl.pallas_call(functools.partial(kernel, sizes, n_slabs), out_shape=jax.S...  67.9 us
    unnamed x11, local copies, waits for them, and re-layouts  4.28 us

profile of v1, /device:TPU:1, one launch (start us, length us, event | category | flops | bytes accessed | tf_op | source)
XLA Modules:
  0.0 72.2 jit_solution(15459273789540087397)
XLA Ops:
  0.0 0.0 copy-start.4
  0.0 0.0 copy-start.3
  0.0 0.7 copy-done.4
  0.7 0.0 copy-done.3
  0.7 0.0 copy-start
  0.7 1.2 %copy-done = f32[1,2,128,1024]{3,2,1,0:T(8,128)S(1)} copy-done((f32[1,2,128,1024]{3,2,1,0:T(8,128)S(1)}, f32[1,2,128,1024]{3,2,1,0:T(8,128)}, u32[]{:S(2)}) %copy-start) | copy-done | bytes 1048600
  1.9 0.0 copy-start.1
  1.9 0.7 copy-done.1
  2.6 0.0 copy-start.2
  2.6 0.7 copy-done.2
  3.3 67.9 %shard_map.55 = f32[2,128,1024]{2,1,0:T(8,128)S(1)} custom-call(f32[2,128,1024]{2,1,0:T(8,128)S(1)} %bitcast.3, f32[2,1024]{1,0:T(2,128)S(1)} %copy-done.1, f32[2,1024]{1,0:T(2,128)S(1)} %copy-done.2, f32[2,3]{1,0:T(2,128)S(1)} %copy-done.3, s32[2]{0:T(128)S(1)} %copy-done.4), custom_call_target="tpu_custom_call" | custom-call | tf_op jit(solution)/shard_map/pallas_call | solution.py:397
  71.3 1.0 %copy.7 = f32[1,2,128,1024]{3,2,1,0:T(8,128)} copy(f32[1,2,128,1024]{3,2,1,0:T(8,128)S(1)} %bitcast.2) | data formatting | bytes 2097152
Async XLA Ops:
  0.0 0.7 copy-start.4
  0.0 0.7 copy-start.3
  0.7 1.2 %copy-start = (f32[1,2,128,1024]{3,2,1,0:T(8,128)S(1)}, f32[1,2,128,1024]{3,2,1,0:T(8,128)}, u32[]{:S(2)}) copy-start(f32[1,2,128,1024]{3,2,1,0:T(8,128)} %param.5) | copy-start | bytes 3145732
  1.9 0.7 copy-start.1
  2.6 0.7 copy-start.2

commit v2 on v1

--- a/solution.py
+++ b/solution.py
@@ -39,7 +39,7 @@
     sizes, n_slabs, x_hbm, one_hbm, two_hbm, taps_hbm, dils_hbm, o_ref,
     x_ref, one_ref, two_ref, taps, dils, send, recv, back, roots_s, roots_r, first, second, gain,
     above, below, kx_high, kx_low, trans, ends, ends2, starts,
-    load_sem, root_sem, halo_sem, out_sem, in_sem, trans_sem, end_sem, end2_sem, home_s, home_r,
+    load_sem, ready_sem, root_sem, halo_sem, out_sem, in_sem, trans_sem, end_sem, end2_sem, home_s, home_r,
 ):
     ny, nz, nxx, nc = sizes
     chips = ny * nxx
@@ -102,7 +102,11 @@
     def hello(gz, slab):
         pl.semaphore_signal(barrier, inc=1, device_id=(gz, slab), device_id_type=MESH)
 
-    hello(partner, gy)
+    leads = half == 0
+
+    @pl.when(leads)
+    def _():
+        hello(partner, gy)
 
     @pl.when(has_up)
     def _():
@@ -144,8 +148,12 @@
         to_flat(1, p, middle[32:])
 
     pl.semaphore_wait(
-        barrier, group + has_up.astype(jnp.int32) + has_down.astype(jnp.int32)
+        barrier, group - 1 + half + has_up.astype(jnp.int32) + has_down.astype(jnp.int32)
     )
+
+    @pl.when(jnp.logical_not(leads))
+    def _():
+        pl.semaphore_signal(ready_sem, inc=1, device_id=(partner, gy), device_id_type=MESH)
 
     for gz, _ in peers(True):
         remote(roots_s, roots_r.at[core, chip], root_sem.at[0], root_sem.at[1], gz).start()
@@ -220,7 +228,10 @@
     trans_copy = remote(
         trans.at[half, chip], trans.at[half, chip], trans_sem.at[0], trans_sem.at[1], partner
     )
-    trans_copy.start()
+
+    @pl.when(jnp.logical_not(leads))
+    def _():
+        trans_copy.start()
 
     @pl.when(has_up)
     def _():
@@ -281,11 +292,18 @@
     def slots(n):
         return range(CHUNKS[n][0], sum(CHUNKS[n]))
 
-    def hand_over(buf, sems, n, scan):
+    def hand_over(buf, sems, n, scan, first_send=False):
         for slot in slots(n):
             for b, (s1, s2) in enumerate(scan(slot, nothing, False)):
                 buf[slot, half, b, 0] = s1
                 buf[slot, half, b, 1] = s2
+        if first_send:
+
+            @pl.when(leads)
+            def _():
+                pl.semaphore_wait(ready_sem, 1)
+                trans_copy.start()
+
         at = pl.ds(*CHUNKS[n])
         remote(
             buf.at[at, half], buf.at[at, half], sems.at[0, n], sems.at[1, n], partner
@@ -309,8 +327,8 @@
 
     for n in range(len(CHUNKS)):
         arrived(recv.at[pl.ds(*CHUNKS[n]), pl.ds(0, 2 * group - 2)], in_sem.at[n])
-        hand_over(ends, end_sem, n, back_scan)
-        if n == 0:
+        hand_over(ends, end_sem, n, back_scan, n == 0)
+        if n == 1:
             trans_copy.wait_recv()
             for gz, _ in peers(True):
                 remote(
@@ -422,6 +440,7 @@
                 vmem((4, nz, ny, 2, 8, 128), F32),
                 vmem((4, nz, ny, 2, 8, 128), F32),
                 dma((5,)),
+                pltpu.SemaphoreType.REGULAR,
                 dma((4,)),
                 dma((4,)),
                 dma((steps,)),
@@ -433,7 +452,7 @@
                 dma((steps,)),
             ],
             compiler_params=pltpu.CompilerParams(
-                collective_id=0, has_side_effects=True, vmem_limit_bytes=48 << 20
+                collective_id=0, has_side_effects=True, vmem_limit_bytes=67043328
             ),
         )(probe_fields[0], root_one, root_two, lateral_kernel_taps, dilations)
         return out[None]

time: 72.5 us -> 65.3 us (0.901)
  the two profiles are of different devices: /device:TPU:1 before, /device:TPU:33 now
where the time goes in v2:
time: 65.3 us; the launch traced here: 65.1 us
  Pallas kernels  62.8 us (96%)
  local copies, waits for them, and re-layouts  2.31 us (4%)
    pallas_call x1, Pallas kernels, body(): pl.pallas_call(functools.partial(kernel, sizes, n_slabs), out_shape=jax.S...  62.8 us
    unnamed x1, local copies, waits for them, and re-layouts  2.31 us

profile of v2, /device:TPU:33, one launch (start us, length us, event | category | flops | bytes accessed | tf_op | source)
XLA Modules:
  0.0 65.1 jit_solution(4487959224654415784)
XLA Ops:
  0.0 62.8 %shard_map.55 = f32[2,128,1024]{2,1,0:T(8,128)} custom-call(f32[2,128,1024]{2,1,0:T(8,128)} %bitcast.3, f32[2,1024]{1,0:T(2,128)} %one_hbm.1, f32[2,1024]{1,0:T(2,128)} %two_hbm.1, f32[2,3]{1,0:T(2,128)} %taps_hbm.1, s32[2]{0:T(128)} %dils_hbm.1), custom_call_target="tpu_custom_call" | custom-call | tf_op jit(solution)/shard_map/pallas_call | solution.py:415
  62.8 2.3 %copy.7 = f32[1,2,128,1024]{3,2,1,0:T(8,128)} copy(f32[1,2,128,1024]{3,2,1,0:T(8,128)} %bitcast.2) | data formatting | bytes 2097152

commit v3 on v2

--- a/solution.py
+++ b/solution.py
@@ -38,8 +38,8 @@
 def kernel(
     sizes, n_slabs, x_hbm, one_hbm, two_hbm, taps_hbm, dils_hbm, o_ref,
     x_ref, one_ref, two_ref, taps, dils, send, recv, back, roots_s, roots_r, first, second, gain,
-    above, below, kx_high, kx_low, trans, ends, ends2, starts,
-    load_sem, ready_sem, root_sem, halo_sem, out_sem, in_sem, trans_sem, end_sem, end2_sem, home_s, home_r,
+    above, below, kx_high, kx_low, entry, trans, ends, ends2, starts,
+    load_sem, ready_sem, row_sem, root_sem, share_sem, halo_sem, out_sem, in_sem, trans_sem, end_sem, end2_sem, home_s, home_r,
 ):
     ny, nz, nxx, nc = sizes
     chips = ny * nxx
@@ -62,9 +62,9 @@
     steps = [(a, b, c) for a in range(ny) for b in range(nxx) for c in range(nc)][1:]
     steps.sort(key=lambda s: (-reach(ny, s[0]) - reach(nxx, s[1]), -min(s[0], 1) - min(s[1], 1)))
 
-    def peers(same_core=False):
+    def peers(kind="all"):
         for a, b, c in steps:
-            if same_core and c:
+            if not {"all": True, "row": a == 0, "core": a and not c, "alike": not c}[kind]:
                 continue
             yy, xx, cc = lax.rem(line + a, ny), lax.rem(col + b, nxx), lax.rem(core + c, nc)
             yield gz_of(yy, half, xx, cc), (yy * nxx + xx) * nc + cc
@@ -155,8 +155,11 @@
     def _():
         pl.semaphore_signal(ready_sem, inc=1, device_id=(partner, gy), device_id_type=MESH)
 
-    for gz, _ in peers(True):
+    for gz, _ in peers("row"):
+        remote(roots_s, roots_r.at[core, chip], row_sem.at[0], row_sem.at[1], gz).start()
+    for gz, _ in peers("core"):
         remote(roots_s, roots_r.at[core, chip], root_sem.at[0], root_sem.at[1], gz).start()
+    roots_r[core, chip] = roots_s[...]
     up = remote(x_ref.at[:, 0:32], below, halo_sem.at[0], halo_sem.at[2], g, gy - 1)
     down = remote(x_ref.at[:, 96:128], above, halo_sem.at[1], halo_sem.at[3], g, gy + 1)
 
@@ -179,59 +182,57 @@
 
     inner_chunks = [n for n, (s, _) in enumerate(CHUNKS) if s < 2]
     outer_chunks = [n for n, (s, _) in enumerate(CHUNKS) if s >= 2]
-    for n in inner_chunks:
-        spread_rows(n)
-    roots_r[core, chip] = roots_s[...]
+    spread_rows(inner_chunks[0])
 
     i = lax.broadcasted_iota(jnp.int32, (256, 128), 0)
     j = lax.broadcasted_iota(jnp.int32, (256, 128), 1)
     kx = stencil(jnp.abs(jnp.where(i < 192, i, i - 256) - j), taps, 0, dils[0])
     kx_high[...], kx_low[...] = pieces(kx)
 
-    arrived(roots_r.at[0, pl.ds(0, chips - 1)], root_sem.at[1])
-    root_copy = remote(
-        roots_r.at[core], roots_r.at[core], root_sem.at[2], root_sem.at[3], sibling
-    )
-    root_copy.start()
-
     head, tail = ky(32, 64), ky(64, 96)
     mid = lax.broadcasted_iota(jnp.int32, (64, 96), 0)
     top = pieces(exact(head, jnp.where(has_up | (mid >= MARGIN), tail, 0.0)))
     bottom = pieces(exact(head, jnp.where(has_down | (mid < 64 - MARGIN), tail, 0.0)))
 
-    root_copy.wait_recv()
-
-    @pl.loop(0, 2 * group)
-    def _(k):
-        c, ch, p = lax.rem(k // 2, nc), k // (2 * nc), lax.rem(k, 2)
-        one, two = roots_r[c, ch, p, 0], roots_r[c, ch, p, 1]
-        first[k], second[k] = one + two, -one * two
-        gain[k] = (1.0 - one) * (1.0 - two)
-
-    def advance(k, states):
-        out = []
-        for b in range(ny):
-            at = b * block + k
-            f, s = first[at], second[at]
-            out.append(tuple((f * y1 + s * y2, y1) for y1, y2 in states[b]))
-        return tuple(out)
-
-    begin = []
-    for b in range(ny):
-        f0, s0, f1, s1 = first[b * block], second[b * block], first[b * block + 1], second[b * block + 1]
-        begin.append(((f1 * f0 + s1, f0), (f1 * s0, s0)))
-    done = lax.fori_loop(2, block, advance, tuple(begin))
-    for b in range(ny):
-        (a, c), (d, e) = done[b]
-        for n, value in enumerate((a, d, c, e)):
-            trans[half, 4 * b + n] = value
+    def transition(roots_of):
+        (f0, s0), (f, s) = (
+            (one + two, -one * two) for one, two in (roots_of(0), roots_of(1))
+        )
+        y = [(f * f0 + s, f0), (f * s0, s0)]
+        for k in range(2, block):
+            one, two = roots_of(k)
+            f, s = one + two, -one * two
+            y = [(f * y1 + s * y2, y1) for y1, y2 in y]
+        (a, c), (d, e) = y
+        return a, d, c, e
+
+    def roots_at(row):
+        def of(k):
+            c, ch, p = k // 2 % nc, row * nxx + k // (2 * nc), k % 2
+            return roots_r[c, ch, p, 0], roots_r[c, ch, p, 1]
+
+        return of
+
+    arrived(roots_r.at[0, pl.ds(0, nxx * nc - 1)], row_sem.at[1])
+    for n, value in enumerate(transition(roots_at(line))):
+        entry[n] = value
     trans_copy = remote(
-        trans.at[half, chip], trans.at[half, chip], trans_sem.at[0], trans_sem.at[1], partner
+        entry.at[col], trans.at[half, chip], trans_sem.at[0], trans_sem.at[1], partner
     )
 
     @pl.when(jnp.logical_not(leads))
     def _():
         trans_copy.start()
+
+    arrived(roots_r.at[0, pl.ds(0, chips - nxx)], root_sem.at[1])
+    root_copies = []
+    for n in range(1, ny):
+        other = roots_r.at[core, pl.ds(lax.rem(line + n, ny) * nxx, nxx)]
+        root_copies.append(remote(other, other, share_sem.at[0, n - 1], share_sem.at[1, n - 1], sibling))
+    for copy in root_copies:
+        copy.start()
+    for n in inner_chunks[1:]:
+        spread_rows(n)
 
     @pl.when(has_up)
     def _():
@@ -252,13 +253,25 @@
     for p in range(2):
         over = jnp.concatenate([above[p], x_ref[p, 0:64]], 0)
         to_flat(2, p, dot3(top, pieces(over)))
-    for n in outer_chunks[:1]:
-        if len(outer_chunks) == 2:
-            spread_rows(n)
+    if len(outer_chunks) == 2:
+        spread_rows(outer_chunks[0])
     for p in range(2):
         under = jnp.concatenate([x_ref[p, 64:128], below[p]], 0)
         to_flat(3, p, dot3(bottom, pieces(under)))
     spread_rows(outer_chunks[-1])
+
+    for copy in root_copies:
+        copy.wait_recv()
+
+    for ch in range(chips):
+        for c in range(nc):
+            one, two = roots_r[c, ch, :, 0], roots_r[c, ch, :, 1]
+            at = pl.ds(2 * (nc * ch + c), 2)
+            first[at], second[at] = one + two, -one * two
+            gain[at] = (1.0 - one) * (1.0 - two)
+    for b in range(ny):
+        for n, value in enumerate(transition(roots_at(b))):
+            trans[half, 4 * b + n] = value
 
     def back_scan(slot, begin, keep):
         def step(i, states):
@@ -330,7 +343,7 @@
         hand_over(ends, end_sem, n, back_scan, n == 0)
         if n == 1:
             trans_copy.wait_recv()
-            for gz, _ in peers(True):
+            for gz, _ in peers("alike"):
                 remote(
                     trans.at[1 - half, chip], trans.at[1 - half, chip],
                     trans_sem.at[2], trans_sem.at[3], gz,
@@ -393,9 +406,11 @@
         down.wait_send()
 
     trans_copy.wait_send()
-    root_copy.wait_send()
+    for copy in root_copies:
+        copy.wait_send()
     arrived(trans.at[1 - half, pl.ds(0, chips - 1)], trans_sem.at[2])
-    arrived(roots_r.at[0, pl.ds(0, chips - 1)], root_sem.at[0])
+    arrived(roots_r.at[0, pl.ds(0, nxx * nc - 1)], row_sem.at[0])
+    arrived(roots_r.at[0, pl.ds(0, chips - nxx)], root_sem.at[0])
     for n in range(len(CHUNKS)):
         at = pl.ds(*CHUNKS[n])
         arrived(send.at[at, :, pl.ds(0, (group - 1) * EIGHTHS)], out_sem.at[n])
@@ -435,13 +450,16 @@
                 vmem((2, 32, 1024), F32),
                 vmem((256, 128), BF16),
                 vmem((256, 128), BF16),
+                vmem((4, 8, 128), F32),
                 vmem((nz, 4 * ny, 8, 128), F32),
                 vmem((4, nz, ny, 2, 8, 128), F32),
                 vmem((4, nz, ny, 2, 8, 128), F32),
                 vmem((4, nz, ny, 2, 8, 128), F32),
                 dma((5,)),
                 pltpu.SemaphoreType.REGULAR,
-                dma((4,)),
+                dma((2,)),
+                dma((2,)),
+                dma((2, ny - 1)),
                 dma((4,)),
                 dma((steps,)),
                 dma((steps,)),
@@ -452,9 +470,14 @@
                 dma((steps,)),
             ],
             compiler_params=pltpu.CompilerParams(
-                collective_id=0, has_side_effects=True, vmem_limit_bytes=67043328
+                collective_id=0, has_side_effects=True, vmem_limit_bytes=48 << 20
             ),
-        )(probe_fields[0], root_one, root_two, lateral_kernel_taps, dilations)
+        )(
+            *(
+                pltpu.with_memory_space_constraint(a, pltpu.HBM)
+                for a in (probe_fields[0], root_one, root_two, lateral_kernel_taps, dilations)
+            )
+        )
         return out[None]
 
     return body

time: 65.3 us -> 66.1 us (1.012)
  Pallas kernels: 62.8 us -> 65 us
  local copies, waits for them, and re-layouts: 2.31 us -> 0.97 us
    pallas_call x1, Pallas kernels: 62.8 us -> 65 us  [body(): pl.pallas_call(functools.partial(kernel, sizes, n_slabs), out_shape=jax.S...]
    unnamed x1, local copies, waits for them, and re-layouts: 2.31 us -> 0.97 us
where the time goes in v3:
time: 66.1 us; the launch traced here: 65.9 us
  Pallas kernels  65 us (98%)
  local copies, waits for them, and re-layouts  0.97 us (1%)
    pallas_call x1, Pallas kernels, body(): pl.pallas_call(functools.partial(kernel, sizes, n_slabs), out_shape=jax.S...  65 us

profile of v3, /device:TPU:33, one launch (start us, length us, event | category | flops | bytes accessed | tf_op | source)
XLA Modules:
  0.0 65.9 jit_solution(4729031868089879865)
XLA Ops:
  0.0 65.0 %shard_map.55 = f32[2,128,1024]{2,1,0:T(8,128)S(1)} custom-call(f32[2,128,1024]{2,1,0:T(8,128)} %bitcast.3, f32[2,1024]{1,0:T(2,128)} %one_hbm.1, f32[2,1024]{1,0:T(2,128)} %two_hbm.1, f32[2,3]{1,0:T(2,128)} %taps_hbm.1, s32[2]{0:T(128)} %dils_hbm.1), custom_call_target="tpu_custom_call" | custom-call | tf_op jit(solution)/shard_map/pallas_call | solution.py:430
  65.0 1.0 %copy.7 = f32[1,2,128,1024]{3,2,1,0:T(8,128)} copy(f32[1,2,128,1024]{3,2,1,0:T(8,128)S(1)} %bitcast.2) | data formatting | bytes 2097152

commit v4 on v3

--- a/solution.py
+++ b/solution.py
@@ -38,7 +38,7 @@
 def kernel(
     sizes, n_slabs, x_hbm, one_hbm, two_hbm, taps_hbm, dils_hbm, o_ref,
     x_ref, one_ref, two_ref, taps, dils, send, recv, back, roots_s, roots_r, first, second, gain,
-    above, below, kx_high, kx_low, entry, trans, ends, ends2, starts,
+    above, below, kx_high, kx_low, entry, trans, ends, ends2,
     load_sem, ready_sem, row_sem, root_sem, share_sem, halo_sem, out_sem, in_sem, trans_sem, end_sem, end2_sem, home_s, home_r,
 ):
     ny, nz, nxx, nc = sizes
@@ -258,7 +258,12 @@
     for p in range(2):
         under = jnp.concatenate([x_ref[p, 64:128], below[p]], 0)
         to_flat(3, p, dot3(bottom, pieces(under)))
-    spread_rows(outer_chunks[-1])
+
+    @pl.when(leads)
+    def _():
+        spread_rows(outer_chunks[-1])
+        pl.semaphore_wait(ready_sem, 1)
+        trans_copy.start()
 
     for copy in root_copies:
         copy.wait_recv()
@@ -305,22 +310,26 @@
     def slots(n):
         return range(CHUNKS[n][0], sum(CHUNKS[n]))
 
-    def hand_over(buf, sems, n, scan, first_send=False):
+    def part(buf, n, z):
+        if buf is ends:
+            blocks = pl.ds(1, ny - 1) if z == 0 else pl.ds(0, ny)
+        else:
+            blocks = pl.ds(0, ny - 1) if z == nz - 1 else pl.ds(0, ny)
+        return buf.at[pl.ds(*CHUNKS[n]), z, blocks]
+
+    def state_sems(buf):
+        return end_sem if buf is ends else end2_sem
+
+    def far_states(buf, n, z):
+        arrived(part(buf, n, 1 - z), state_sems(buf).at[1, n])
+
+    def hand_over(buf, n, z, scan):
         for slot in slots(n):
             for b, (s1, s2) in enumerate(scan(slot, nothing, False)):
-                buf[slot, half, b, 0] = s1
-                buf[slot, half, b, 1] = s2
-        if first_send:
-
-            @pl.when(leads)
-            def _():
-                pl.semaphore_wait(ready_sem, 1)
-                trans_copy.start()
-
-        at = pl.ds(*CHUNKS[n])
-        remote(
-            buf.at[at, half], buf.at[at, half], sems.at[0, n], sems.at[1, n], partner
-        ).start()
+                buf[slot, z, b, 0] = s1
+                buf[slot, z, b, 1] = s2
+        states, sems = part(buf, n, z), state_sems(buf)
+        remote(states, states, sems.at[0, n], sems.at[1, n], partner).start()
 
     def x_twice(slot):
         n = 2 * group * EIGHTHS
@@ -335,49 +344,55 @@
             own = dot3(pieces(jnp.concatenate([own, sides], 1)), matrix)
         recv[slot] = own.reshape(2 * group, EIGHTHS, 128)
 
-    def far_state(buf, n):
-        arrived(buf.at[pl.ds(*CHUNKS[n]), 1 - half], (end_sem if buf is ends else end2_sem).at[1, n])
-
-    for n in range(len(CHUNKS)):
+    def take_in(n, z):
         arrived(recv.at[pl.ds(*CHUNKS[n]), pl.ds(0, 2 * group - 2)], in_sem.at[n])
-        hand_over(ends, end_sem, n, back_scan, n == 0)
-        if n == 1:
-            trans_copy.wait_recv()
-            for gz, _ in peers("alike"):
-                remote(
-                    trans.at[1 - half, chip], trans.at[1 - half, chip],
-                    trans_sem.at[2], trans_sem.at[3], gz,
-                ).start()
-
-    arrived(trans.at[1 - half, pl.ds(0, chips - 1)], trans_sem.at[3])
-
-    for n in range(len(CHUNKS)):
-        far_state(ends, n)
+        hand_over(ends, n, z, back_scan)
+
+    def pass_on():
+        trans_copy.wait_recv()
+        for gz, _ in peers("alike"):
+            remote(
+                trans.at[1 - half, chip], trans.at[1 - half, chip],
+                trans_sem.at[2], trans_sem.at[3], gz,
+            ).start()
+
+    def have_transitions():
+        arrived(trans.at[1 - half, pl.ds(0, chips - 1)], trans_sem.at[3])
+
+    def middle(n, mine):
+        far_states(ends, n, mine)
         for slot in slots(n):
             u, t = zero, zero
+            begin = [None] * ny
             for j in reversed(range(ny * nz)):
                 b, z = j // nz, j % nz
-                starts[slot, z, b, 0], starts[slot, z, b, 1] = u, t
-                a11, a12, a21, a22 = (trans[z, 4 * b + i] for i in range(4))
-                u, t = a11 * u + a21 * t + ends[slot, z, b, 0], a12 * u + a22 * t + ends[slot, z, b, 1]
-            begin = [(starts[slot, half, b, 0], starts[slot, half, b, 1]) for b in range(ny)]
+                if z == mine:
+                    begin[b] = (u, t)
+                if j:
+                    a11, a12, a21, a22 = (trans[z, 4 * b + i] for i in range(4))
+                    u, t = (
+                        a11 * u + a21 * t + ends[slot, z, b, 0],
+                        a12 * u + a22 * t + ends[slot, z, b, 1],
+                    )
             back_scan(slot, begin, True)
             x_twice(slot)
-        hand_over(ends2, end2_sem, n, fore_scan)
-
-    for n in range(len(CHUNKS)):
-        far_state(ends2, n)
+        hand_over(ends2, n, mine, fore_scan)
+
+    def finish(n, mine):
+        far_states(ends2, n, mine)
         for slot in slots(n):
             y1, y2 = zero, zero
+            begin = [None] * ny
             for j in range(ny * nz):
                 b, z = j // nz, j % nz
-                starts[slot, z, b, 0], starts[slot, z, b, 1] = y1, y2
-                a11, a12, a21, a22 = (trans[z, 4 * b + i] for i in range(4))
-                y1, y2 = (
-                    a11 * y1 + a12 * y2 + ends2[slot, z, b, 0],
-                    a21 * y1 + a22 * y2 + ends2[slot, z, b, 1],
-                )
-            begin = [(starts[slot, half, b, 0], starts[slot, half, b, 1]) for b in range(ny)]
+                if z == mine:
+                    begin[b] = (y1, y2)
+                if j < ny * nz - 1:
+                    a11, a12, a21, a22 = (trans[z, 4 * b + i] for i in range(4))
+                    y1, y2 = (
+                        a11 * y1 + a12 * y2 + ends2[slot, z, b, 0],
+                        a21 * y1 + a22 * y2 + ends2[slot, z, b, 1],
+                    )
             fore_scan(slot, begin, True)
         at = pl.ds(*CHUNKS[n])
         for gz, place in peers():
@@ -386,6 +401,42 @@
                 home_s.at[n], home_r.at[n], gz,
             ).start()
         back[at, :, flat(me)] = recv[at, pl.ds(2 * me, 2)]
+
+    def sent(z):
+        for n in range(len(CHUNKS)):
+            for buf in (ends, ends2):
+                arrived(part(buf, n, z), state_sems(buf).at[0, n])
+
+    last = len(CHUNKS)
+
+    @pl.when(leads)
+    def _():
+        for n in range(last):
+            take_in(n, 0)
+        pass_on()
+        have_transitions()
+        for n in range(last):
+            middle(n, 0)
+            if n:
+                finish(n - 1, 0)
+        finish(last - 1, 0)
+        sent(0)
+
+    @pl.when(jnp.logical_not(leads))
+    def _():
+        take_in(0, 1)
+        pass_on()
+        spread_rows(outer_chunks[-1])
+        take_in(1, 1)
+        have_transitions()
+        for n in range(2, last):
+            middle(n - 2, 1)
+            take_in(n, 1)
+        for n in range(last - 2, last):
+            middle(n, 1)
+        for n in range(last):
+            finish(n, 1)
+        sent(1)
 
     for n in range(len(CHUNKS)):
         arrived(back.at[pl.ds(*CHUNKS[n]), :, pl.ds(0, (group - 1) * EIGHTHS)], home_r.at[n])
@@ -414,8 +465,6 @@
     for n in range(len(CHUNKS)):
         at = pl.ds(*CHUNKS[n])
         arrived(send.at[at, :, pl.ds(0, (group - 1) * EIGHTHS)], out_sem.at[n])
-        arrived(ends.at[at, 0], end_sem.at[0, n])
-        arrived(ends2.at[at, 0], end2_sem.at[0, n])
         arrived(back.at[at, :, pl.ds(0, (group - 1) * EIGHTHS)], home_s.at[n])
 
 
@@ -454,7 +503,6 @@
                 vmem((nz, 4 * ny, 8, 128), F32),
                 vmem((4, nz, ny, 2, 8, 128), F32),
                 vmem((4, nz, ny, 2, 8, 128), F32),
-                vmem((4, nz, ny, 2, 8, 128), F32),
                 dma((5,)),
                 pltpu.SemaphoreType.REGULAR,
                 dma((2,)),

time: 66.1 us -> 62.7 us (0.949)
  the two profiles are of different devices: /device:TPU:33 before, /device:TPU:35 now
where the time goes in v4:
time: 62.7 us; the launch traced here: 62.6 us
  Pallas kernels  61.6 us (98%)
  local copies, waits for them, and re-layouts  0.97 us (2%)
    pallas_call x1, Pallas kernels, body(): pl.pallas_call(functools.partial(kernel, sizes, n_slabs), out_shape=jax.S...  61.6 us

profile of v4, /device:TPU:35, one launch (start us, length us, event | category | flops | bytes accessed | tf_op | source)
XLA Modules:
  0.0 62.6 jit_solution(8704619872760008465)
XLA Ops:
  0.0 61.6 %shard_map.55 = f32[2,128,1024]{2,1,0:T(8,128)S(1)} custom-call(f32[2,128,1024]{2,1,0:T(8,128)} %bitcast.3, f32[2,1024]{1,0:T(2,128)} %one_hbm.1, f32[2,1024]{1,0:T(2,128)} %two_hbm.1, f32[2,3]{1,0:T(2,128)} %taps_hbm.1, s32[2]{0:T(128)} %dils_hbm.1), custom_call_target="tpu_custom_call" | custom-call | tf_op jit(solution)/shard_map/pallas_call | solution.py:479
  61.6 1.0 %copy.7 = f32[1,2,128,1024]{3,2,1,0:T(8,128)} copy(f32[1,2,128,1024]{3,2,1,0:T(8,128)S(1)} %bitcast.2) | data formatting | bytes 2097152

commit v5 on v4

--- a/solution.py
+++ b/solution.py
@@ -38,7 +38,7 @@
 def kernel(
     sizes, n_slabs, x_hbm, one_hbm, two_hbm, taps_hbm, dils_hbm, o_ref,
     x_ref, one_ref, two_ref, taps, dils, send, recv, back, roots_s, roots_r, first, second, gain,
-    above, below, kx_high, kx_low, entry, trans, ends, ends2,
+    above, below, kx_both, entry, trans, ends, ends2,
     load_sem, ready_sem, row_sem, root_sem, share_sem, halo_sem, out_sem, in_sem, trans_sem, end_sem, end2_sem, home_s, home_r,
 ):
     ny, nz, nxx, nc = sizes
@@ -187,7 +187,7 @@
     i = lax.broadcasted_iota(jnp.int32, (256, 128), 0)
     j = lax.broadcasted_iota(jnp.int32, (256, 128), 1)
     kx = stencil(jnp.abs(jnp.where(i < 192, i, i - 256) - j), taps, 0, dils[0])
-    kx_high[...], kx_low[...] = pieces(kx)
+    kx_both[:, :128], kx_both[:, 128:] = pieces(kx)
 
     head, tail = ky(32, 64), ky(64, 96)
     mid = lax.broadcasted_iota(jnp.int32, (64, 96), 0)
@@ -332,17 +332,20 @@
         remote(states, states, sems.at[0, n], sems.at[1, n], partner).start()
 
     def x_twice(slot):
-        n = 2 * group * EIGHTHS
-        eighth = lax.rem(lax.broadcasted_iota(jnp.int32, (n, 128), 0), EIGHTHS)
-        lane = lax.broadcasted_iota(jnp.int32, (n, 128), 1)
-        own = recv[slot].reshape(n, 128)
-        matrix = (kx_high[...], kx_low[...])
+        n = 2 * group
+        eighth = lax.broadcasted_iota(jnp.int32, (n, EIGHTHS, 128), 1)
+        lane = lax.broadcasted_iota(jnp.int32, (n, EIGHTHS, 128), 2)
+        own = recv[slot]
         for _ in range(2):
-            before = jnp.where(eighth == 0, 0.0, pltpu.roll(own, 1, 0))
-            after = jnp.where(eighth == EIGHTHS - 1, 0.0, pltpu.roll(own, n - 1, 0))
+            before = jnp.where(eighth == 0, 0.0, pltpu.roll(own, 1, 1))
+            after = jnp.where(eighth == EIGHTHS - 1, 0.0, pltpu.roll(own, EIGHTHS - 1, 1))
             sides = jnp.where(lane < 64, after, before)
-            own = dot3(pieces(jnp.concatenate([own, sides], 1)), matrix)
-        recv[slot] = own.reshape(2 * group, EIGHTHS, 128)
+            both = jnp.concatenate([own, sides], 2).reshape(n * EIGHTHS, 256)
+            high, low = pieces(both)
+            wide = jnp.dot(high, kx_both[...], preferred_element_type=F32)
+            rest = jnp.dot(low, kx_both[:, :128], preferred_element_type=F32)
+            own = (wide[:, :128] + (wide[:, 128:] + rest)).reshape(n, EIGHTHS, 128)
+        recv[slot] = own
 
     def take_in(n, z):
         arrived(recv.at[pl.ds(*CHUNKS[n]), pl.ds(0, 2 * group - 2)], in_sem.at[n])
@@ -497,8 +500,7 @@
                 vmem((2 * group, 8, 128), F32),
                 vmem((2, 32, 1024), F32),
                 vmem((2, 32, 1024), F32),
-                vmem((256, 128), BF16),
-                vmem((256, 128), BF16),
+                vmem((256, 256), BF16),
                 vmem((4, 8, 128), F32),
                 vmem((nz, 4 * ny, 8, 128), F32),
                 vmem((4, nz, ny, 2, 8, 128), F32),

time: 62.7 us -> 62.4 us (level)
  no operation moved by 1% of the time
where the time goes in v5:
time: 62.4 us; the launch traced here: 62.2 us
  Pallas kernels  61.2 us (98%)
  local copies, waits for them, and re-layouts  0.97 us (2%)
    pallas_call x1, Pallas kernels, body(): pl.pallas_call(functools.partial(kernel, sizes, n_slabs), out_shape=jax.S...  61.2 us

profile of v5, /device:TPU:35, one launch (start us, length us, event | category | flops | bytes accessed | tf_op | source)
XLA Modules:
  0.0 62.2 jit_solution(14966272657761778114)
XLA Ops:
  0.0 61.2 %shard_map.55 = f32[2,128,1024]{2,1,0:T(8,128)S(1)} custom-call(f32[2,128,1024]{2,1,0:T(8,128)} %bitcast.3, f32[2,1024]{1,0:T(2,128)} %one_hbm.1, f32[2,1024]{1,0:T(2,128)} %two_hbm.1, f32[2,3]{1,0:T(2,128)} %taps_hbm.1, s32[2]{0:T(128)} %dils_hbm.1), custom_call_target="tpu_custom_call" | custom-call | tf_op jit(solution)/shard_map/pallas_call | solution.py:482
  61.3 1.0 %copy.7 = f32[1,2,128,1024]{3,2,1,0:T(8,128)} copy(f32[1,2,128,1024]{3,2,1,0:T(8,128)S(1)} %bitcast.2) | data formatting | bytes 2097152
